TPU v7x, 32 devices: a whole 2x2x4 slice. The times are simulated.
32 devices in a mesh: group: 2 (over y), batch: 4 (over z), expert: 4 (over x, core).
Axes of the slice: x: 2, y: 2, z: 4, core: 2. Of those that a mesh axis runs over, the one named last changes fastest.
Arguments:
- residual_in: bfloat16 [128, 4096], P(('group', 'batch')), parts along dimension 0, may hold values from -11 to 11
- queries: bfloat16 [128, 16, 128], P(('group', 'batch'), 'expert'), parts along dimension 0, may hold values from -150 to 150
- key_new: bfloat16 [128, 4, 128], P(('group', 'batch'), 'expert'), parts along dimension 0, may hold values from -6 to 6
- value_new: bfloat16 [128, 4, 128], P(('group', 'batch'), 'expert'), parts along dimension 0, may hold values from -6 to 6
- key_cache: bfloat16 [128, 4, 256, 128], P(('group', 'batch'), 'expert'), parts along dimension 0, may hold values from -6 to 6
- value_cache: bfloat16 [128, 4, 256, 128], P(('group', 'batch'), 'expert'), parts along dimension 0, may hold values from -6 to 6
- cache_len: int32 [128], P(('group', 'batch')), parts along dimension 0, may hold values from 1 to 256, 8192 in all
- new_slot: int32 [128], P(('group', 'batch')), parts along dimension 0, may hold values 0 or 1
- out_weight: bfloat16 [2048, 4096], P('expert'), may hold values from -0.125 to 0.125
- norm_gain: float32 [4096], replicated, may hold values from 0.5 to 1.5
- router: bfloat16 [4096, 4], replicated, may hold values from -0.09375 to 0.09375
- chosen: int32 [128, 2], P(('group', 'batch')), parts along dimension 0, may hold values from 0 to 3, all different within a row; in each aligned block of 16 rows (0 to 15, 16 to 31, ...) at most 12 rows name the same one
- w_gate: bfloat16 [4, 4096, 8192], P('expert', None, 'batch'), may hold values from -0.09375 to 0.09375
- w_up: bfloat16 [4, 4096, 8192], P('expert', None, 'batch'), may hold values from -0.09375 to 0.09375
- w_down: bfloat16 [4, 8192, 4096], P('expert', 'batch'), may hold values from -0.0625 to 0.0625
Outputs:
- layer_out: bfloat16 [128, 4096], P(('group', 'batch', 'expert')), parts along dimension 0
There are 2 independent parts, one for each index of `group`. A program takes and returns all parts, laid end to end along the dimension named above; an argument that names none is the same for every part. Nothing has to cross between parts.
Inputs may be any that keep to these rules, and one draw needn't show every extreme that they name: `chosen`: each row names 2 different experts. Among the rows of one device no expert is named by more than 12 rows, and in every draw some expert is named by exactly 12 rows of some device. `cache_len`: the lengths of a part sum to 8192, and the largest is exactly 256.
All inputs are finite; a program needn't handle non-finite values. No bound on the sum of `cache_len` or of `new_slot` on one device may be relied on, other than what follows from the above.
Results may differ from a plain program's by a relative error of at most 0.017.
Values may be sent and summed in bfloat16 or wider, within the bound.
A program may use at most 128 MiB of HBM per device.

v0:
```python
import jax
import jax.numpy as jnp
from jax import lax
from jax.sharding import PartitionSpec as P

CAP = 12


epsilon = 1e-05


def attend(queries, key_new, value_new, key_cache, value_cache, cache_len, new_slot):
    slot_count, kv_count, length, head_width = key_cache.shape
    group_size = queries.shape[1] // kv_count
    grouped = queries.reshape(slot_count, kv_count, group_size, head_width)
    scaling = float(head_width) ** (-0.5)
    scores = (
        jnp.einsum("skgd,sktd->skgt", grouped, key_cache, preferred_element_type=jnp.float32)
        * scaling
    )
    own_score = (
        jnp.einsum("skgd,skd->skg", grouped, key_new, preferred_element_type=jnp.float32) * scaling
    )
    places = lax.broadcasted_iota(jnp.int32, (slot_count, length), 1)
    usable = (places < cache_len[:, None]) & (new_slot[:, None] == 0)
    usable = usable[:, None, None, :]
    scores = jnp.where(usable, scores, jnp.float32(-1e30))
    highest = jnp.maximum(jnp.max(scores, axis=3), own_score)
    weights = jnp.where(usable, jnp.exp(scores - highest[..., None]), jnp.float32(0.0))
    own_weight = jnp.exp(own_score - highest)
    denominator = jnp.sum(weights, axis=3) + own_weight
    probabilities = (weights / denominator[..., None]).astype(jnp.bfloat16)
    own_prob = (own_weight / denominator).astype(jnp.bfloat16)
    attended = jnp.einsum(
        "skgt,sktd->skgd", probabilities, value_cache, preferred_element_type=jnp.float32
    )
    attended = (
        attended
        + own_prob.astype(jnp.float32)[..., None] * value_new.astype(jnp.float32)[:, :, None, :]
    )
    return attended.reshape(slot_count, kv_count * group_size * head_width).astype(jnp.bfloat16)


def mixing(logits, chosen, expert_count):
    labels = lax.broadcasted_iota(jnp.int32, (1, 1, expert_count), 2)
    picking = (chosen[:, :, None] == labels).astype(jnp.float32)
    chosen_logits = jnp.sum(picking * logits[:, None, :], axis=2)
    leading = jax.nn.sigmoid(chosen_logits[:, 0] - chosen_logits[:, 1])
    fractions = jnp.stack([leading, 1.0 - leading], axis=1)
    return jnp.sum(picking * fractions[:, :, None], axis=1)


def placement_table(chosen, targets, capacity):
    routed = jnp.sum((chosen[None, :, :] == targets[:, None, None]).astype(jnp.int32), axis=2)
    position = jnp.cumsum(routed, axis=1) - routed
    row_labels = lax.broadcasted_iota(jnp.int32, (1, capacity, 1), 1)
    return ((position[:, None, :] == row_labels) & (routed[:, None, :] == 1)).astype(jnp.float32)


def body(
    residual_in,
    queries,
    key_new,
    value_new,
    key_cache,
    value_cache,
    cache_len,
    new_slot,
    out_weight,
    norm_gain,
    router,
    chosen,
    w_gate,
    w_up,
    w_down,
):
    my_expert = lax.axis_index("expert")
    attended = attend(queries, key_new, value_new, key_cache, value_cache, cache_len, new_slot)
    partial_value = jnp.dot(attended, out_weight, preferred_element_type=jnp.float32)
    summed = lax.psum(partial_value, "expert")
    stream = (residual_in.astype(jnp.float32) + summed).astype(jnp.bfloat16)
    values = stream.astype(jnp.float32)
    scaling = lax.rsqrt(jnp.mean(values * values, axis=1, keepdims=True) + epsilon)
    normed = (values * scaling * norm_gain).astype(jnp.bfloat16)
    logits = jnp.dot(normed, router, preferred_element_type=jnp.float32)
    placing = placement_table(chosen, jnp.reshape(my_expert, (1,)), CAP)[0]
    sent_rows = jnp.dot(
        placing.astype(jnp.bfloat16), normed, preferred_element_type=jnp.float32
    ).astype(jnp.bfloat16)
    carried = values * (my_expert == 0).astype(jnp.float32)
    coef = mixing(logits, chosen, router.shape[1])
    expert_labels = lax.broadcasted_iota(jnp.int32, (1, router.shape[1]), 1)
    my_coef = jnp.sum(coef * (expert_labels == my_expert).astype(jnp.float32), axis=1)
    row_weight = jnp.dot(placing, my_coef, precision=lax.Precision.HIGHEST)
    block_rows = lax.all_gather(sent_rows, "batch", axis=0, tiled=True)
    gate_part = jnp.dot(block_rows, w_gate[0], preferred_element_type=jnp.float32)
    up_part = jnp.dot(block_rows, w_up[0], preferred_element_type=jnp.float32)
    hidden = (jax.nn.silu(gate_part) * up_part).astype(jnp.bfloat16)
    block_rows = hidden
    outputs = lax.psum_scatter(
        jnp.dot(block_rows, w_down[0], preferred_element_type=jnp.float32).astype(jnp.bfloat16),
        "batch",
        scatter_dimension=0,
        tiled=True,
    ).astype(jnp.float32)
    weighted = row_weight[:, None] * outputs
    contribution = jnp.dot(placing.T, weighted, precision=lax.Precision.HIGHEST) + carried
    layer_out = lax.psum_scatter(
        contribution.astype(jnp.bfloat16), "expert", scatter_dimension=0, tiled=True
    )
    return layer_out


def solution(mesh):
    in_specs = (
        P(("group", "batch"), None),
        P(("group", "batch"), "expert", None),
        P(("group", "batch"), "expert", None),
        P(("group", "batch"), "expert", None),
        P(("group", "batch"), "expert", None, None),
        P(("group", "batch"), "expert", None, None),
        P(("group", "batch")),
        P(("group", "batch")),
        P("expert", None),
        P(),
        P(),
        P(("group", "batch"), None),
        P("expert", None, "batch"),
        P("expert", None, "batch"),
        P("expert", "batch", None),
    )
    out_specs = P(("group", "batch", "expert"), None)
    return jax.shard_map(body, mesh=mesh, in_specs=in_specs, out_specs=out_specs, check_vma=False)
```

profile of v0, /device:TPU:0, one launch (start us, length us, event | category | flops | bytes accessed | tf_op | source)
XLA Modules:
  0.0 154.4 jit_solution(7242869067965577408)
XLA Ops:
  6.5 0.0 copy-start
  6.5 0.0 all-reduce.6.cloned.1.call-start
  6.5 0.7 broadcast_compare_fusion
  7.3 0.7 fusion.48
  8.0 0.9 fusion.52
  8.9 0.0 copy-done
  8.9 1.2 fusion.67
  10.1 0.2 fusion.37
  10.3 0.7 bitcast_convert_fusion
  11.0 1.5 fusion.19
  12.5 3.6 %fusion.45 = f32[16,4096]{1,0:T(8,128)} fusion(bf16[512,4096]{1,0:T(8,128)(2,1)} %param.23, bf16[2,8,4,128]{3,2,1,0:T(4,128)(2,1)S(1)} %bitcast.56), kind=kOutput, calls=%fused_computation.45 | convolution fusion | flops 67108864 | bytes 4472832 | tf_op jit(solution)/shard_map/dot_general | solution.py:79
  16.1 0.0 all-reduce.6.cloned.1.call-update
  16.1 0.0 all-reduce.8.cloned.1.call-start
  16.1 0.7 fusion.63
  16.8 0.1 copy.26
  17.0 0.1 reduce.6
  17.1 1.2 dynamic-slice.6
  19.0 32.2 %all-reduce.6.cloned.1.call-done = f32[16,4096]{1,0:T(8,128)} async-done(((f32[16,4096]{1,0:T(8,128)}), f32[16,4096]{1,0:T(8,128)}) %all-reduce.6.cloned.1.call-update) | async-done | bytes 262160 | tf_op jit(solution)/shard_map/psum | solution.py:80
  51.2 1.1 fusion.29
  52.4 1.0 fusion.11
  53.3 15.2 %all-gather = bf16[4,12,4096]{2,1,0:T(8,128)(2,1)S(1)} all-gather(bf16[1,12,4096]{2,1,0:T(8,128)(2,1)S(1)} %fusion.11), channel_id=1, replica_groups=mesh['group'=2,'batch'=4,'expert'=4] {'batch'}, dimensions={0}, use_global_device_ids=true | all-gather | bytes 491520 | tf_op jit(solution)/shard_map/all_gather | solution.py:95
  68.5 0.1 reshape.221
  68.6 8.8 %fusion.5 = f32[48,2048]{1,0:T(8,128)S(1)} fusion(bf16[48,4096]{1,0:T(8,128)(2,1)S(1)} %reshape.221, bf16[1,4096,2048]{2,1,0:T(8,128)(2,1)} %param.27), kind=kOutput, calls=%fused_computation.4 | convolution fusion | flops 805306368 | bytes 17563648 | tf_op jit(solution)/shard_map/dot_general | solution.py:96
  77.4 0.0 copy-start.1
  77.4 0.0 copy-start.3
  77.4 0.0 copy-start.2
  77.4 0.0 copy-start.4
  77.5 13.7 %fusion.7 = bf16[48,4096]{1,0:T(8,128)(2,1)S(1)} fusion(bf16[1,2048,4096]{2,1,0:T(8,128)(2,1)} %param.29, bf16[48,4096]{1,0:T(8,128)(2,1)S(1)} %reshape.221, bf16[1,4096,2048]{2,1,0:T(8,128)(2,1)} %param.28, f32[48,2048]{1,0:T(8,128)S(1)} %fusion.5), kind=kOutput, calls=%fused_computation.6 | convolution fusion | flops 1611399168 | bytes 34734080 | tf_op jit(solution)/shard_map/dot_general | solution.py:101
  91.1 16.0 %fusion = bf16[16,4096]{1,0:T(8,128)(2,1)S(1)} fusion(bf16[48,4096]{1,0:T(8,128)(2,1)S(1)} %fusion.7), kind=kCustom, calls=%all-reduce-scatter | all-reduce-scatter fusion | flops 262145 | bytes 524800
  107.2 2.8 %collective-permute-start = (bf16[12,4096]{1,0:T(8,128)(2,1)S(1)}, bf16[12,4096]{1,0:T(8,128)(2,1)S(1)}, u32[]{:S(2)}, u32[]{:S(2)}) collective-permute-start(bf16[12,4096]{1,0:T(8,128)(2,1)S(1)} %slice.8), channel_id=1, source_target_pairs={{0,4},{4,8},{8,12},{1,5},{5,9},{9,13},{2,6},{6,10},{10,14},{3,7},{... | collective-permute-start | bytes 294920
  110.0 0.0 copy-done.1
  110.1 0.0 copy-done.3
  110.1 0.2 fusion.43
  110.3 0.0 copy-done.2
  110.4 0.1 multiply_reduce_fusion
  110.5 0.1 convolution_bitcast_fusion
  110.6 2.0 %collective-permute-done = bf16[12,4096]{1,0:T(8,128)(2,1)S(1)} collective-permute-done((bf16[12,4096]{1,0:T(8,128)(2,1)S(1)}, bf16[12,4096]{1,0:T(8,128)(2,1)S(1)}, u32[]{:S(2)}, u32[]{:S(2)}) %collective-permute-start) | collective-permute-done | bytes 98336
  112.5 0.3 concatenate
  112.9 1.0 fusion.10
  113.9 0.0 all-reduce.8.cloned.1.call-update
  113.9 0.0 copy-done.4
  113.9 0.6 dynamic-slice.2
  115.1 31.0 %all-reduce.8.cloned.1.call-done = bf16[16,4096]{1,0:T(8,128)(2,1)} async-done(((bf16[16,4096]{1,0:T(8,128)(2,1)}), bf16[16,4096]{1,0:T(8,128)(2,1)}) %all-reduce.8.cloned.1.call-update) | async-done | bytes 131088
  146.1 1.5 constant_dynamic-slice_fusion
  (12 shorter events, 0.2 us)
Async XLA Ops:
  6.5 2.3 %copy-start = (bf16[16,1,256,128]{3,2,1,0:T(8,128)(2,1)S(1)}, bf16[16,1,256,128]{3,2,1,0:T(8,128)(2,1)}, u32[]{:S(2)}) copy-start(bf16[16,1,256,128]{3,2,1,0:T(8,128)(2,1)} %param.19) | copy-start | bytes 3145732
  6.5 44.7 %all-reduce.6.cloned.1.call-start = ((), (), s32[]{:S(2)}) async-start(), calls=%async_computation | async-start | bytes 524288 | tf_op jit(solution)/shard_map/psum | solution.py:80
  16.1 130.0 %all-reduce.8.cloned.1.call-start = ((), (), s32[]{:S(2)}) async-start(), calls=%async_computation.1 | async-start | bytes 262144
  77.4 32.6 %copy-start.1 = (f32[4096]{0:T(1024)S(1)}, f32[4096]{0:T(1024)}, u32[]{:S(2)}) copy-start(f32[4096]{0:T(1024)} %param.24) | copy-start | bytes 49156
  77.4 32.6 %copy-start.3 = (bf16[4096,4]{0,1:T(4,128)(2,1)S(1)}, bf16[4096,4]{0,1:T(4,128)(2,1)}, u32[]{:S(2)}) copy-start(bf16[4096,4]{0,1:T(4,128)(2,1)} %param.25) | copy-start | bytes 98308
  77.4 32.9 %copy-start.2 = (s32[16,2]{0,1:T(2,128)S(1)}, s32[16,2]{0,1:T(2,128)}, u32[]{:S(2)}) copy-start(s32[16,2]{0,1:T(2,128)} %param.26) | copy-start | bytes 388
  77.4 36.4 %copy-start.4 = (u32[32]{0:T(128)S(1)}, u32[32]{0:T(128)}, u32[]{:S(2)}) copy-start(u32[32]{0:T(128)} %constant.45) | copy-start | bytes 388
  107.2 5.4 %collective-permute-start = (bf16[12,4096]{1,0:T(8,128)(2,1)S(1)}, bf16[12,4096]{1,0:T(8,128)(2,1)S(1)}, u32[]{:S(2)}, u32[]{:S(2)}) collective-permute-start(bf16[12,4096]{1,0:T(8,128)(2,1)S(1)} %slice.8), channel_id=1, source_target_pairs={{0,4},{4,8},{8,12},{1,5},{5,9},{9,13},{2,6},{6,10},{10,14},{3,7},{... | collective-permute-start | bytes 294920
Sparse Core Ops, SparseCore 0:
  16.2 34.9 all-reduce.5
  114.0 32.0 all-reduce.7
where the time goes:
time: 155 us; the launch traced here: 154 us
  waiting for transfers between devices  65.2 us (42%)
  matrix products  31.9 us (21%)
  blocking collectives  31.2 us (20%)
  between operations  14.9 us (10%)
  other arithmetic  4.53 us (3%)
  local copies, waits for them, and re-layouts  3.85 us (2%)
  starting transfers between devices  2.89 us (2%)
    unnamed x4, waiting for transfers between devices  33 us
    psum x1, waiting for transfers between devices, body(): summed = lax.psum(partial_value, 'expert')  32.2 us
    unnamed x1, blocking collectives  16 us
    all_gather x1, blocking collectives, body(): block_rows = lax.all_gather(sent_rows, 'batch', axis=0, tiled=True)  15.2 us
    dot_general x1, matrix products, body(): jnp.dot(block_rows, w_down[0], preferred_element_type=jnp.float32)  13.7 us
    dot_general x1, matrix products, body(): jnp.dot(block_rows, w_gate[0], preferred_element_type=jnp.float32)  8.79 us
    unnamed x16, local copies, waits for them, and re-layouts  3.76 us
    dot_general x1, matrix products, body(): jnp.dot(attended, out_weight, preferred_element_type=jnp.float32)  3.56 us
  transfers between devices with their start and end apart: 3, of which 3 were waited for; matrix products, arithmetic and copies ran while one was open for 2% of the time, Pallas kernels for 0%

commit v1 on v0

v1 whole, which is shorter than its diff:
```python
import functools

import jax
import jax.numpy as jnp
from jax import lax
from jax.experimental import pallas as pl
from jax.experimental.pallas import tpu as pltpu
from jax.sharding import PartitionSpec as P

EPS = 1e-05
MESH = pl.DeviceIdType.MESH
PAD = 128


def chunk_of(extent, wanted):
    return wanted if extent % wanted == 0 else extent


def kernel(
    nb, ne,
    lens, fresh, chosen,
    resid_h, q_h, kn_h, vn_h, k_h, v_h, wo_h, gain_h, router_h, wg_h, wu_h, wd_h,
    out,
    resid, q, kn, vn, k, v, wo, gain, router, wg, wu, wd,
    scores, own, att, part, resid_rows, part_in, msg, msg_in, rows32, x, hidden,
    y, y_in, mine, z, z_in, stream_s,
    small_sem, wo_sem, gate_sem, up_sem, down_sem,
    ra_s, ra_r, ba_s, ba_r, xa_s, xa_r, ya_s, ya_r, za_s, za_r,
):
    slots, heads, width = q.shape
    length = k.shape[1]
    dim = wo.shape[1]
    hid = wg.shape[1]
    own_rows = slots // ne
    block = nb * own_rows
    g = lax.axis_index("group")
    b = lax.axis_index("batch")
    e = lax.axis_index("expert")
    wo_n, hid_n, down_n = wo_sem.shape[0], gate_sem.shape[0], down_sem.shape[0]
    wo_c, hid_c, down_c = dim // wo_n, hid // hid_n, dim // down_n

    small = [
        pltpu.make_async_copy(src, dst, small_sem.at[i])
        for i, (src, dst) in enumerate([
            (q_h, q), (kn_h, kn), (k_h.at[:, 0], k), (vn_h, vn), (v_h.at[:, 0], v),
            (resid_h, resid), (gain_h, gain), (router_h, router),
        ])
    ]
    for copy in small:
        copy.start()
    wo_copies = []
    for i in range(wo_n):
        cols = pl.ds(i * wo_c, wo_c)
        wo_copies.append(pltpu.make_async_copy(wo_h.at[:, cols], wo.at[:, cols], wo_sem.at[i]))
        wo_copies[-1].start()

    def gate_copy(i):
        cols = pl.ds(pl.multiple_of(i * hid_c, hid_c), hid_c)
        return pltpu.make_async_copy(wg_h.at[0, :, cols], wg.at[:, cols], gate_sem.at[i])

    def up_copy(i):
        cols = pl.ds(pl.multiple_of(i * hid_c, hid_c), hid_c)
        return pltpu.make_async_copy(wu_h.at[0, :, cols], wu.at[:, cols], up_sem.at[i])

    for i in range(hid_n):
        gate_copy(i).start()
        up_copy(i).start()
    down_copies = []
    for i in range(down_n):
        cols = pl.ds(i * down_c, down_c)
        down_copies.append(pltpu.make_async_copy(wd_h.at[0, :, cols], wd.at[:, cols], down_sem.at[i]))
        down_copies[-1].start()

    def expert_peer(j):
        return (g, b, lax.rem(e + j, ne))

    def batch_peer(j):
        return (g, lax.rem(b + j, nb), e)

    barrier = pltpu.get_barrier_semaphore()
    for j in range(1, ne):
        pl.semaphore_signal(barrier, inc=1, device_id=expert_peer(j), device_id_type=MESH)
    for j in range(1, nb):
        pl.semaphore_signal(barrier, inc=1, device_id=batch_peer(j), device_id_type=MESH)

    scale = float(width) ** (-0.5)
    for i in (0, 1, 2):
        small[i].wait()
    places = lax.broadcasted_iota(jnp.int32, (heads, length), 1)
    for s in range(slots):
        used = jnp.where(fresh[s] == 0, lens[s], 0)
        at = pl.ds(s * heads, heads)
        c = lax.dot_general(q[s], k[s], (((1,), (1,)), ((), ())), preferred_element_type=jnp.float32)
        scores[at, :] = jnp.where(places < used, c * scale, jnp.float32(-1e30))
        o = jnp.sum(q[s].astype(jnp.float32) * kn[s].astype(jnp.float32), axis=1, keepdims=True)
        own[at, :] = jnp.broadcast_to(o * scale, (heads, own.shape[1]))
    c = scores[...]
    o = own[:, 0:1]
    highest = jnp.maximum(jnp.max(c, axis=1, keepdims=True), o)
    weights = jnp.exp(c - highest)
    own_weight = jnp.exp(o - highest)
    total = jnp.sum(weights, axis=1, keepdims=True) + own_weight
    scores[...] = weights / total
    own[...] = jnp.broadcast_to(own_weight / total, own.shape)
    for i in (3, 4):
        small[i].wait()
    for s in range(slots):
        at = pl.ds(s * heads, heads)
        a = jnp.dot(scores[at, :].astype(jnp.bfloat16), v[s], preferred_element_type=jnp.float32)
        own_prob = own[at, :].astype(jnp.bfloat16).astype(jnp.float32)
        att[at, :] = a + own_prob * vn[s].astype(jnp.float32)
    attended = jnp.concatenate(
        [att[pl.ds(h, slots, stride=heads), :] for h in range(heads)], axis=1
    ).astype(jnp.bfloat16)

    pl.semaphore_wait(barrier, ne - 1 + nb - 1)
    for i in range(wo_n):
        wo_copies[i].wait()
        cols = pl.ds(i * wo_c, wo_c)
        p = jnp.dot(attended, wo[:, cols], preferred_element_type=jnp.float32)
        for j in range(ne):
            part[j, :, cols] = p[j * own_rows:(j + 1) * own_rows].astype(jnp.bfloat16)
    part_copies = []
    for j in range(1, ne):
        part_copies.append(pltpu.make_async_remote_copy(
            src_ref=part.at[lax.rem(e + j, ne)], dst_ref=part_in.at[j - 1],
            send_sem=ra_s.at[j - 1], recv_sem=ra_r.at[j - 1],
            device_id=expert_peer(j), device_id_type=MESH))
        part_copies[-1].start()
    for i in (5, 6, 7):
        small[i].wait()
    r32 = resid[...].astype(jnp.float32)
    for j in range(ne):
        resid_rows[j] = r32[j * own_rows:(j + 1) * own_rows]
    summed = part[e].astype(jnp.float32)
    for j in range(1, ne):
        part_copies[j - 1].wait()
        summed = summed + part_in[j - 1].astype(jnp.float32)
    values = (resid_rows[e] + summed).astype(jnp.bfloat16).astype(jnp.float32)
    stream_s[...] = values
    norm = lax.rsqrt(jnp.mean(values * values, axis=1, keepdims=True) + EPS)
    normed = (values * norm * gain[...]).astype(jnp.bfloat16)
    msg[:, 0:dim] = normed
    n32 = normed.astype(jnp.float32)
    lane = lax.broadcasted_iota(jnp.int32, (own_rows, PAD), 1)
    row = lax.broadcasted_iota(jnp.int32, (own_rows, PAD), 0)
    logits = jnp.zeros((own_rows, PAD), jnp.float32)
    for j in range(ne):
        l = jnp.sum(n32 * router[j:j + 1, :].astype(jnp.float32), axis=1, keepdims=True)
        logits = jnp.where(lane == j, l, logits)
    first = jnp.zeros((own_rows, PAD), jnp.int32)
    second = jnp.zeros((own_rows, PAD), jnp.int32)
    for i in range(own_rows):
        first = jnp.where(row == i, chosen[e * own_rows + i, 0], first)
        second = jnp.where(row == i, chosen[e * own_rows + i, 1], second)
    la = jnp.sum(jnp.where(lane == first, logits, 0.0), axis=1, keepdims=True)
    lb = jnp.sum(jnp.where(lane == second, logits, 0.0), axis=1, keepdims=True)
    ca = 1.0 / (1.0 + jnp.exp(lb - la))
    coef = jnp.where(lane == first, ca, jnp.where(lane == second, 1.0 - ca, 0.0))
    high = coef.astype(jnp.bfloat16)
    msg[:, dim:dim + PAD] = high
    msg[:, dim + PAD:dim + 2 * PAD] = (coef - high.astype(jnp.float32)).astype(jnp.bfloat16)

    msg_copies = []
    for j in range(1, nb):
        msg_copies.append(pltpu.make_async_remote_copy(
            src_ref=msg, dst_ref=msg_in.at[j - 1],
            send_sem=ba_s.at[j - 1], recv_sem=ba_r.at[j - 1],
            device_id=batch_peer(j), device_id_type=MESH))
        msg_copies[-1].start()
    rows32[0:own_rows, :] = msg[...].astype(jnp.float32)
    for j in range(1, nb):
        msg_copies[j - 1].wait()
        rows32[j * own_rows:(j + 1) * own_rows, :] = msg_in[j - 1].astype(jnp.float32)
    x[0:block, :] = rows32[...].astype(jnp.bfloat16)
    x_copies = []
    for j in range(1, ne):
        x_copies.append(pltpu.make_async_remote_copy(
            src_ref=x.at[pl.ds(0, block)], dst_ref=x.at[pl.ds(j * block, block)],
            send_sem=xa_s.at[j - 1], recv_sem=xa_r.at[j - 1],
            device_id=expert_peer(j), device_id_type=MESH))
        x_copies[-1].start()
    for copy in x_copies:
        copy.wait()

    def gate_up(i, carry):
        gate_copy(i).wait()
        up_copy(i).wait()
        cols = pl.ds(pl.multiple_of(i * hid_c, hid_c), hid_c)
        gp = jnp.dot(x[:, 0:dim], wg[:, cols], preferred_element_type=jnp.float32)
        up = jnp.dot(x[:, 0:dim], wu[:, cols], preferred_element_type=jnp.float32)
        hidden[:, cols] = (gp / (1.0 + jnp.exp(-gp)) * up).astype(jnp.bfloat16)
        return carry

    lax.fori_loop(0, hid_n, gate_up, 0)

    lanes = lax.broadcasted_iota(jnp.int32, (ne * block, PAD), 1)
    both = x[:, dim:dim + PAD].astype(jnp.float32) + x[:, dim + PAD:dim + 2 * PAD].astype(jnp.float32)
    my_coef = jnp.sum(jnp.where(lanes == e, both, 0.0), axis=1, keepdims=True)

    y_copies, z_copies = [], []

    def forward(n):
        cols = pl.ds(n * down_c, down_c)
        acc = y[n, 0:block, :].astype(jnp.float32)
        for j in range(1, ne):
            y_copies[n][j - 1].wait()
            acc = acc + y_in[n, j - 1].astype(jnp.float32)
        mine[:, cols] = acc[0:own_rows]
        sent = []
        for j in range(1, nb):
            z[n, j - 1] = acc[j * own_rows:(j + 1) * own_rows].astype(jnp.bfloat16)
        for j in range(1, nb):
            sent.append(pltpu.make_async_remote_copy(
                src_ref=z.at[n, j - 1], dst_ref=z_in.at[n, j - 1],
                send_sem=za_s.at[n, j - 1], recv_sem=za_r.at[n, j - 1],
                device_id=batch_peer(nb - j), device_id_type=MESH))
            sent[-1].start()
        z_copies.append(sent)

    def finish(n):
        cols = pl.ds(n * down_c, down_c)
        acc = stream_s[:, cols] + mine[:, cols]
        for j in range(1, nb):
            z_copies[n][j - 1].wait()
            acc = acc + z_in[n, j - 1].astype(jnp.float32)
        out[:, cols] = acc.astype(jnp.bfloat16)

    for n in range(down_n):
        cols = pl.ds(n * down_c, down_c)
        down_copies[n].wait()
        d = jnp.dot(hidden[...], wd[:, cols], preferred_element_type=jnp.float32)
        y[n] = (d * my_coef).astype(jnp.bfloat16)
        sent = []
        for j in range(1, ne):
            sent.append(pltpu.make_async_remote_copy(
                src_ref=y.at[n, pl.ds(j * block, block)], dst_ref=y_in.at[n, j - 1],
                send_sem=ya_s.at[n, j - 1], recv_sem=ya_r.at[n, j - 1],
                device_id=expert_peer(ne - j), device_id_type=MESH))
            sent[-1].start()
        y_copies.append(sent)
        if n > 0:
            forward(n - 1)
    forward(down_n - 1)
    for n in range(down_n):
        finish(n)


def body(nb, ne, residual_in, queries, key_new, value_new, key_cache, value_cache,
         cache_len, new_slot, out_weight, norm_gain, router, chosen, w_gate, w_up, w_down):
    slots, heads, width = queries.shape
    length = key_cache.shape[2]
    feat, dim = out_weight.shape
    hid = w_gate.shape[2]
    own_rows = slots // ne
    block = nb * own_rows
    wo_n = dim // chunk_of(dim, 1024)
    hid_n = hid // chunk_of(hid, 256)
    down_n = dim // chunk_of(dim, 1024)
    down_c = dim // down_n
    bf, f32 = jnp.bfloat16, jnp.float32
    smem = pl.BlockSpec(memory_space=pltpu.SMEM)
    anywhere = pl.BlockSpec(memory_space=pl.ANY)
    dma = pltpu.SemaphoreType.DMA
    ext = dim + 2 * PAD
    return pl.pallas_call(
        functools.partial(kernel, nb, ne),
        out_shape=jax.ShapeDtypeStruct((own_rows, dim), bf),
        in_specs=[smem] * 3 + [anywhere] * 12,
        out_specs=pl.BlockSpec(memory_space=pltpu.VMEM),
        scratch_shapes=[
            pltpu.VMEM((slots, dim), bf),
            pltpu.VMEM((slots, heads, width), bf),
            pltpu.VMEM((slots, 1, width), bf),
            pltpu.VMEM((slots, 1, width), bf),
            pltpu.VMEM((slots, length, width), bf),
            pltpu.VMEM((slots, length, width), bf),
            pltpu.VMEM((feat, dim), bf),
            pltpu.VMEM((1, dim), f32),
            pltpu.VMEM((ne, dim), bf),
            pltpu.VMEM((dim, hid), bf),
            pltpu.VMEM((dim, hid), bf),
            pltpu.VMEM((hid, dim), bf),
            pltpu.VMEM((slots * heads, length), f32),
            pltpu.VMEM((slots * heads, width), f32),
            pltpu.VMEM((slots * heads, width), f32),
            pltpu.VMEM((ne, own_rows, dim), bf),
            pltpu.VMEM((ne, own_rows, dim), f32),
            pltpu.VMEM((ne - 1, own_rows, dim), bf),
            pltpu.VMEM((own_rows, ext), bf),
            pltpu.VMEM((nb - 1, own_rows, ext), bf),
            pltpu.VMEM((block, ext), f32),
            pltpu.VMEM((ne * block, ext), bf),
            pltpu.VMEM((ne * block, hid), bf),
            pltpu.VMEM((down_n, ne * block, down_c), bf),
            pltpu.VMEM((down_n, ne - 1, block, down_c), bf),
            pltpu.VMEM((own_rows, dim), f32),
            pltpu.VMEM((down_n, nb - 1, own_rows, down_c), bf),
            pltpu.VMEM((down_n, nb - 1, own_rows, down_c), bf),
            pltpu.VMEM((own_rows, dim), f32),
            dma((8,)), dma((wo_n,)), dma((hid_n,)), dma((hid_n,)), dma((down_n,)),
            dma((ne - 1,)), dma((ne - 1,)), dma((nb - 1,)), dma((nb - 1,)),
            dma((ne - 1,)), dma((ne - 1,)),
            dma((down_n, ne - 1)), dma((down_n, ne - 1)),
            dma((down_n, nb - 1)), dma((down_n, nb - 1)),
        ],
        compiler_params=pltpu.CompilerParams(
            collective_id=0, has_side_effects=True, vmem_limit_bytes=67043328
        ),
    )(
        cache_len, new_slot, chosen, residual_in, queries, key_new, value_new, key_cache,
        value_cache, out_weight, norm_gain.reshape(1, dim), router.T, w_gate, w_up, w_down,
    )


def solution(mesh):
    in_specs = (
        P(("group", "batch"), None),
        P(("group", "batch"), "expert", None),
        P(("group", "batch"), "expert", None),
        P(("group", "batch"), "expert", None),
        P(("group", "batch"), "expert", None, None),
        P(("group", "batch"), "expert", None, None),
        P(("group", "batch")),
        P(("group", "batch")),
        P("expert", None),
        P(),
        P(),
        P(("group", "batch"), None),
        P("expert", None, "batch"),
        P("expert", None, "batch"),
        P("expert", "batch", None),
    )
    out_specs = P(("group", "batch", "expert"), None)
    return jax.shard_map(
        functools.partial(body, mesh.shape["batch"], mesh.shape["expert"]),
        mesh=mesh, in_specs=in_specs, out_specs=out_specs, check_vma=False,
    )
```

time: 155 us -> 61.7 us (0.40)
  waiting for transfers between devices: 65.2 us -> 0 us
  Pallas kernels: 0 us -> 56 us
  matrix products: 31.9 us -> 0 us
  blocking collectives: 31.2 us -> 0 us
  between operations: 14.9 us -> 0.01 us
  other arithmetic: 4.53 us -> 0 us
  starting transfers between devices: 2.89 us -> 0 us
    pallas_call x0 -> x1, Pallas kernels: none -> 56 us  [body(): pl.pallas_call(functools.partial(kernel, nb, ne), out_shape=jax.ShapeDtyp...]
    unnamed x4 -> x0, waiting for transfers between devices: 33 us -> none
    psum x1 -> x0, waiting for transfers between devices: 32.2 us -> none  [body(): summed = lax.psum(partial_value, 'expert')]
    dot_general x10 -> x0, matrix products: 31.9 us -> none  [the longest x1 13.7 us: body(): jnp.dot(block_rows, w_down[0], preferred_element_type=jnp.float32)]
    unnamed x1 -> x0, blocking collectives: 16 us -> none
    all_gather x1 -> x0, blocking collectives: 15.2 us -> none  [body(): block_rows = lax.all_gather(sent_rows, 'batch', axis=0, tiled=True)]
    unnamed x2 -> x0, starting transfers between devices: 2.89 us -> none
    reduce_sum x6 -> x0, other arithmetic: 2.14 us -> none  [the longest x1 1.13 us: body(): jnp.mean(values * values, axis=1, keepdims=True) + epsilon]
  transfers between devices with their start and end apart: 3 -> 0, of which waited for: 3 -> 0; matrix products, arithmetic and copies ran while one was open for 2% -> 0% of each run, Pallas kernels for 0% -> 0%
where the time goes in v1:
time: 61.7 us; the launch traced here: 61.4 us
  Pallas kernels  56 us (91%)
  local copies, waits for them, and re-layouts  5.31 us (9%)
    pallas_call x1, Pallas kernels, body(): pl.pallas_call(functools.partial(kernel, nb, ne), out_shape=jax.ShapeDtyp...  56 us
    unnamed x4, local copies, waits for them, and re-layouts  5.31 us

profile of v1, /device:TPU:0, one launch (start us, length us, event | category | flops | bytes accessed | tf_op | source)
XLA Modules:
  0.0 61.4 jit_solution(16913705690303644466)
XLA Ops:
  0.0 1.3 %copy.17.kn_h = bf16[16,1,128]{2,1,0:T(2,128)(2,1)} copy(bf16[16,1,128]{2,0,1:T(8,128)(2,1)} %param.17) | data formatting | bytes 8192 | tf_op args[2]
  1.3 1.3 %copy.18.vn_h = bf16[16,1,128]{2,1,0:T(2,128)(2,1)} copy(bf16[16,1,128]{2,0,1:T(8,128)(2,1)} %param.18) | data formatting | bytes 8192 | tf_op args[3]
  2.6 1.4 %copy.16.chosen = s32[16,2]{1,0:T(8,128)} copy(s32[16,2]{0,1:T(2,128)} %param.26) | data formatting | bytes 256 | tf_op args[11]
  3.9 56.0 %shard_map.145 = bf16[4,4096]{1,0:T(4,128)(2,1)} custom-call(s32[16]{0:T(128)} %lens.1, s32[16]{0:T(128)} %fresh.1, s32[16,2]{1,0:T(8,128)} %copy.16.chosen, bf16[16,4096]{1,0:T(8,128)(2,1)} %resid_h.1, bf16[16,4,128]{2,1,0:T(4,128)(2,1)} %q_h.1, bf16[16,1,128]{2,1,0:T(2,128)(2,1)} %copy.17.kn_h, bf16[16,1,128]{2,1,0:T(2,128)(2,1)} %copy.18.vn_h, ...), custom_call_target="tpu_custom_call" | custom-call | tf_op jit(solution)/shard_map/pallas_call | solution.py:266
  60.0 1.4 %copy.20 = bf16[4,4096]{1,0:T(4,128)(2,1)} copy(bf16[4,4096]{1,0:T(4,128)(2,1)} %shard_map.145) | data formatting | bytes 65536

commit v2 on v1

--- a/solution.py
+++ b/solution.py
@@ -63,13 +63,13 @@
         return pltpu.make_async_copy(wu_h.at[0, :, cols], wu.at[:, cols], up_sem.at[i])
 
     for i in range(hid_n):
-        gate_copy(i).start()
-        up_copy(i).start()
+        gate_copy(i).start(priority=1)
+        up_copy(i).start(priority=1)
     down_copies = []
     for i in range(down_n):
         cols = pl.ds(i * down_c, down_c)
         down_copies.append(pltpu.make_async_copy(wd_h.at[0, :, cols], wd.at[:, cols], down_sem.at[i]))
-        down_copies[-1].start()
+        down_copies[-1].start(priority=1)
 
     def expert_peer(j):
         return (g, b, lax.rem(e + j, ne))
@@ -92,7 +92,7 @@
         at = pl.ds(s * heads, heads)
         c = lax.dot_general(q[s], k[s], (((1,), (1,)), ((), ())), preferred_element_type=jnp.float32)
         scores[at, :] = jnp.where(places < used, c * scale, jnp.float32(-1e30))
-        o = jnp.sum(q[s].astype(jnp.float32) * kn[s].astype(jnp.float32), axis=1, keepdims=True)
+        o = jnp.sum(q[s].astype(jnp.float32) * kn[0, s:s + 1].astype(jnp.float32), axis=1, keepdims=True)
         own[at, :] = jnp.broadcast_to(o * scale, (heads, own.shape[1]))
     c = scores[...]
     o = own[:, 0:1]
@@ -108,7 +108,7 @@
         at = pl.ds(s * heads, heads)
         a = jnp.dot(scores[at, :].astype(jnp.bfloat16), v[s], preferred_element_type=jnp.float32)
         own_prob = own[at, :].astype(jnp.bfloat16).astype(jnp.float32)
-        att[at, :] = a + own_prob * vn[s].astype(jnp.float32)
+        att[at, :] = a + own_prob * vn[0, s:s + 1].astype(jnp.float32)
     attended = jnp.concatenate(
         [att[pl.ds(h, slots, stride=heads), :] for h in range(heads)], axis=1
     ).astype(jnp.bfloat16)
@@ -151,8 +151,8 @@
     first = jnp.zeros((own_rows, PAD), jnp.int32)
     second = jnp.zeros((own_rows, PAD), jnp.int32)
     for i in range(own_rows):
-        first = jnp.where(row == i, chosen[e * own_rows + i, 0], first)
-        second = jnp.where(row == i, chosen[e * own_rows + i, 1], second)
+        first = jnp.where(row == i, chosen[0, e * own_rows + i], first)
+        second = jnp.where(row == i, chosen[1, e * own_rows + i], second)
     la = jnp.sum(jnp.where(lane == first, logits, 0.0), axis=1, keepdims=True)
     lb = jnp.sum(jnp.where(lane == second, logits, 0.0), axis=1, keepdims=True)
     ca = 1.0 / (1.0 + jnp.exp(lb - la))
@@ -271,8 +271,8 @@
         scratch_shapes=[
             pltpu.VMEM((slots, dim), bf),
             pltpu.VMEM((slots, heads, width), bf),
-            pltpu.VMEM((slots, 1, width), bf),
-            pltpu.VMEM((slots, 1, width), bf),
+            pltpu.VMEM((1, slots, width), bf),
+            pltpu.VMEM((1, slots, width), bf),
             pltpu.VMEM((slots, length, width), bf),
             pltpu.VMEM((slots, length, width), bf),
             pltpu.VMEM((feat, dim), bf),
@@ -308,8 +308,8 @@
             collective_id=0, has_side_effects=True, vmem_limit_bytes=67043328
         ),
     )(
-        cache_len, new_slot, chosen, residual_in, queries, key_new, value_new, key_cache,
-        value_cache, out_weight, norm_gain.reshape(1, dim), router.T, w_gate, w_up, w_down,
+        cache_len, new_slot, chosen.T, residual_in, queries, jnp.transpose(key_new, (1, 0, 2)),
+        jnp.transpose(value_new, (1, 0, 2)), key_cache, value_cache, out_weight, norm_gain.reshape(1, dim), router.T, w_gate, w_up, w_down,
     )
 
 

time: 61.7 us -> 46.1 us (0.75)
  Pallas kernels: 56 us -> 44.5 us
  local copies, waits for them, and re-layouts: 5.31 us -> 1.39 us
    pallas_call x1, Pallas kernels: 56 us -> 44.5 us  [body(): pl.pallas_call(functools.partial(kernel, nb, ne), out_shape=jax.ShapeDtyp...]
    unnamed x4 -> x1, local copies, waits for them, and re-layouts: 5.31 us -> 1.39 us
where the time goes in v2:
time: 46.1 us; the launch traced here: 45.8 us
  Pallas kernels  44.5 us (97%)
  local copies, waits for them, and re-layouts  1.39 us (3%)
    pallas_call x1, Pallas kernels, body(): pl.pallas_call(functools.partial(kernel, nb, ne), out_shape=jax.ShapeDtyp...  44.5 us
    unnamed x1, local copies, waits for them, and re-layouts  1.39 us

profile of v2, /device:TPU:0, one launch (start us, length us, event | category | flops | bytes accessed | tf_op | source)
XLA Modules:
  0.0 45.8 jit_solution(18446288975295291616)
XLA Ops:
  0.0 44.5 %shard_map.145 = bf16[4,4096]{1,0:T(4,128)(2,1)} custom-call(s32[16]{0:T(128)} %lens.1, s32[16]{0:T(128)} %fresh.1, s32[2,16]{1,0:T(2,128)} %bitcast.9, bf16[16,4096]{1,0:T(8,128)(2,1)} %resid_h.1, bf16[16,4,128]{2,1,0:T(4,128)(2,1)} %q_h.1, bf16[1,16,128]{2,1,0:T(8,128)(2,1)} %bitcast.7, bf16[1,16,128]{2,1,0:T(8,128)(2,1)} %bitcast.8, ...), custom_call_target="tpu_custom_call" | custom-call | tf_op jit(solution)/shard_map/pallas_call | solution.py:266
  44.5 1.4 %copy.17 = bf16[4,4096]{1,0:T(4,128)(2,1)} copy(bf16[4,4096]{1,0:T(4,128)(2,1)} %shard_map.145) | data formatting | bytes 65536

commit v3 on v2

--- a/solution.py
+++ b/solution.py
@@ -22,10 +22,10 @@
     resid_h, q_h, kn_h, vn_h, k_h, v_h, wo_h, gain_h, router_h, wg_h, wu_h, wd_h,
     out,
     resid, q, kn, vn, k, v, wo, gain, router, wg, wu, wd,
-    scores, own, att, part, resid_rows, part_in, msg, msg_in, rows32, x, hidden,
-    y, y_in, mine, z, z_in, stream_s,
+    scores, own, att, part, resid_rows, part_in, xin, rows32, x, hidden,
+    y, y_in, held, u, u_in, mine, z, z_in, stream_s,
     small_sem, wo_sem, gate_sem, up_sem, down_sem,
-    ra_s, ra_r, ba_s, ba_r, xa_s, xa_r, ya_s, ya_r, za_s, za_r,
+    ra_s, ra_r, ba_s, ba_r, xa_s, xa_r, pa_s, pa_r, ya_s, ya_r, ua_s, ua_r, za_s, za_r,
 ):
     slots, heads, width = q.shape
     length = k.shape[1]
@@ -71,8 +71,18 @@
         down_copies.append(pltpu.make_async_copy(wd_h.at[0, :, cols], wd.at[:, cols], down_sem.at[i]))
         down_copies[-1].start(priority=1)
 
+    low = 2 if ne % 2 == 0 else 1
+    high_n = ne // low
+    eh, el = e // low, lax.rem(e, low)
+
     def expert_peer(j):
         return (g, b, lax.rem(e + j, ne))
+
+    def far_peer(j):
+        return (g, b, lax.rem(eh + j, high_n) * low + el)
+
+    def pair_peer():
+        return (g, b, eh * low + lax.rem(el + 1, low))
 
     def batch_peer(j):
         return (g, lax.rem(b + j, nb), e)
@@ -114,33 +124,36 @@
     ).astype(jnp.bfloat16)
 
     pl.semaphore_wait(barrier, ne - 1 + nb - 1)
+    part_copies = []
     for i in range(wo_n):
         wo_copies[i].wait()
         cols = pl.ds(i * wo_c, wo_c)
         p = jnp.dot(attended, wo[:, cols], preferred_element_type=jnp.float32)
         for j in range(ne):
-            part[j, :, cols] = p[j * own_rows:(j + 1) * own_rows].astype(jnp.bfloat16)
-    part_copies = []
-    for j in range(1, ne):
-        part_copies.append(pltpu.make_async_remote_copy(
-            src_ref=part.at[lax.rem(e + j, ne)], dst_ref=part_in.at[j - 1],
-            send_sem=ra_s.at[j - 1], recv_sem=ra_r.at[j - 1],
-            device_id=expert_peer(j), device_id_type=MESH))
-        part_copies[-1].start()
+            part[i, j] = p[j * own_rows:(j + 1) * own_rows].astype(jnp.bfloat16)
+        for j in range(1, ne):
+            part_copies.append(pltpu.make_async_remote_copy(
+                src_ref=part.at[i, lax.rem(e + j, ne)], dst_ref=part_in.at[i, j - 1],
+                send_sem=ra_s.at[i, j - 1], recv_sem=ra_r.at[i, j - 1],
+                device_id=expert_peer(j), device_id_type=MESH))
+            part_copies[-1].start()
     for i in (5, 6, 7):
         small[i].wait()
     r32 = resid[...].astype(jnp.float32)
     for j in range(ne):
         resid_rows[j] = r32[j * own_rows:(j + 1) * own_rows]
-    summed = part[e].astype(jnp.float32)
-    for j in range(1, ne):
-        part_copies[j - 1].wait()
-        summed = summed + part_in[j - 1].astype(jnp.float32)
-    values = (resid_rows[e] + summed).astype(jnp.bfloat16).astype(jnp.float32)
-    stream_s[...] = values
+    for copy in part_copies:
+        copy.wait()
+    for i in range(wo_n):
+        cols = pl.ds(i * wo_c, wo_c)
+        summed = part[i, e].astype(jnp.float32)
+        for j in range(1, ne):
+            summed = summed + part_in[i, j - 1].astype(jnp.float32)
+        stream_s[:, cols] = (resid_rows[e, :, cols] + summed).astype(jnp.bfloat16).astype(jnp.float32)
+    values = stream_s[...]
     norm = lax.rsqrt(jnp.mean(values * values, axis=1, keepdims=True) + EPS)
     normed = (values * norm * gain[...]).astype(jnp.bfloat16)
-    msg[:, 0:dim] = normed
+    xin[0, 0, :, 0:dim] = normed
     n32 = normed.astype(jnp.float32)
     lane = lax.broadcasted_iota(jnp.int32, (own_rows, PAD), 1)
     row = lax.broadcasted_iota(jnp.int32, (own_rows, PAD), 0)
@@ -158,30 +171,53 @@
     ca = 1.0 / (1.0 + jnp.exp(lb - la))
     coef = jnp.where(lane == first, ca, jnp.where(lane == second, 1.0 - ca, 0.0))
     high = coef.astype(jnp.bfloat16)
-    msg[:, dim:dim + PAD] = high
-    msg[:, dim + PAD:dim + 2 * PAD] = (coef - high.astype(jnp.float32)).astype(jnp.bfloat16)
-
-    msg_copies = []
-    for j in range(1, nb):
-        msg_copies.append(pltpu.make_async_remote_copy(
-            src_ref=msg, dst_ref=msg_in.at[j - 1],
-            send_sem=ba_s.at[j - 1], recv_sem=ba_r.at[j - 1],
-            device_id=batch_peer(j), device_id_type=MESH))
-        msg_copies[-1].start()
-    rows32[0:own_rows, :] = msg[...].astype(jnp.float32)
-    for j in range(1, nb):
-        msg_copies[j - 1].wait()
-        rows32[j * own_rows:(j + 1) * own_rows, :] = msg_in[j - 1].astype(jnp.float32)
-    x[0:block, :] = rows32[...].astype(jnp.bfloat16)
-    x_copies = []
-    for j in range(1, ne):
-        x_copies.append(pltpu.make_async_remote_copy(
-            src_ref=x.at[pl.ds(0, block)], dst_ref=x.at[pl.ds(j * block, block)],
-            send_sem=xa_s.at[j - 1], recv_sem=xa_r.at[j - 1],
-            device_id=expert_peer(j), device_id_type=MESH))
-        x_copies[-1].start()
-    for copy in x_copies:
-        copy.wait()
+    xin[0, 0, :, dim:dim + PAD] = high
+    xin[0, 0, :, dim + PAD:dim + 2 * PAD] = (coef - high.astype(jnp.float32)).astype(jnp.bfloat16)
+
+    def take(s, k):
+        at = (s * nb + k) * own_rows
+        rows32[at:at + own_rows, :] = xin[s, k].astype(jnp.float32)
+
+    def far_copy(j, k):
+        return pltpu.make_async_remote_copy(
+            src_ref=xin.at[0, k], dst_ref=xin.at[j, k],
+            send_sem=xa_s.at[j - 1, k], recv_sem=xa_r.at[j - 1, k],
+            device_id=far_peer(j), device_id_type=MESH)
+
+    def pair_copy(j, k):
+        return pltpu.make_async_remote_copy(
+            src_ref=xin.at[j, k], dst_ref=xin.at[high_n + j, k],
+            send_sem=pa_s.at[j, k], recv_sem=pa_r.at[j, k],
+            device_id=pair_peer(), device_id_type=MESH)
+
+    near_first = sorted(range(nb), key=lambda k: min(k, nb - k))
+    z_rows = {}
+    for k in near_first[1:]:
+        z_rows[k] = pltpu.make_async_remote_copy(
+            src_ref=xin.at[0, 0], dst_ref=xin.at[0, k],
+            send_sem=ba_s.at[k - 1], recv_sem=ba_r.at[k - 1],
+            device_id=batch_peer(k), device_id_type=MESH)
+        z_rows[k].start()
+    for k in near_first:
+        if k > 0:
+            z_rows[k].wait()
+        for j in range(1, high_n):
+            far_copy(j, k).start()
+        if low == 2:
+            pair_copy(0, k).start()
+        take(0, k)
+    for k in near_first:
+        for j in range(1, high_n):
+            far_copy(j, k).wait()
+            if low == 2:
+                pair_copy(j, k).start()
+            take(j, k)
+    if low == 2:
+        for j in range(high_n):
+            for k in near_first:
+                pair_copy(j, k).wait()
+                take(high_n + j, k)
+    x[...] = rows32[...].astype(jnp.bfloat16)
 
     def gate_up(i, carry):
         gate_copy(i).wait()
@@ -198,31 +234,47 @@
     both = x[:, dim:dim + PAD].astype(jnp.float32) + x[:, dim + PAD:dim + 2 * PAD].astype(jnp.float32)
     my_coef = jnp.sum(jnp.where(lanes == e, both, 0.0), axis=1, keepdims=True)
 
-    y_copies, z_copies = [], []
-
-    def forward(n):
+    y_copies, u_copies, z_copies = [], [], []
+    near = high_n * block
+
+    def far_step(n):
+        acc = y[n, 0:near, :].astype(jnp.float32)
+        if low == 2:
+            y_copies[n].wait()
+            acc = acc + y_in[n].astype(jnp.float32)
+        held[n] = acc[0:block]
+        sent = []
+        for j in range(1, high_n):
+            u[n, j - 1] = acc[j * block:(j + 1) * block].astype(jnp.bfloat16)
+            sent.append(pltpu.make_async_remote_copy(
+                src_ref=u.at[n, j - 1], dst_ref=u_in.at[n, j - 1],
+                send_sem=ua_s.at[n, j - 1], recv_sem=ua_r.at[n, j - 1],
+                device_id=far_peer(high_n - j), device_id_type=MESH))
+            sent[-1].start()
+        u_copies.append(sent)
+
+    def batch_step(n):
         cols = pl.ds(n * down_c, down_c)
-        acc = y[n, 0:block, :].astype(jnp.float32)
-        for j in range(1, ne):
-            y_copies[n][j - 1].wait()
-            acc = acc + y_in[n, j - 1].astype(jnp.float32)
+        acc = held[n]
+        for j in range(1, high_n):
+            u_copies[n][j - 1].wait()
+            acc = acc + u_in[n, j - 1].astype(jnp.float32)
         mine[:, cols] = acc[0:own_rows]
-        sent = []
-        for j in range(1, nb):
+        sent = {}
+        for j in sorted(range(1, nb), key=lambda k: -min(k, nb - k)):
             z[n, j - 1] = acc[j * own_rows:(j + 1) * own_rows].astype(jnp.bfloat16)
-        for j in range(1, nb):
-            sent.append(pltpu.make_async_remote_copy(
+            sent[j] = pltpu.make_async_remote_copy(
                 src_ref=z.at[n, j - 1], dst_ref=z_in.at[n, j - 1],
                 send_sem=za_s.at[n, j - 1], recv_sem=za_r.at[n, j - 1],
-                device_id=batch_peer(nb - j), device_id_type=MESH))
-            sent[-1].start()
+                device_id=batch_peer(nb - j), device_id_type=MESH)
+            sent[j].start()
         z_copies.append(sent)
 
     def finish(n):
         cols = pl.ds(n * down_c, down_c)
         acc = stream_s[:, cols] + mine[:, cols]
         for j in range(1, nb):
-            z_copies[n][j - 1].wait()
+            z_copies[n][j].wait()
             acc = acc + z_in[n, j - 1].astype(jnp.float32)
         out[:, cols] = acc.astype(jnp.bfloat16)
 
@@ -231,17 +283,19 @@
         down_copies[n].wait()
         d = jnp.dot(hidden[...], wd[:, cols], preferred_element_type=jnp.float32)
         y[n] = (d * my_coef).astype(jnp.bfloat16)
-        sent = []
-        for j in range(1, ne):
-            sent.append(pltpu.make_async_remote_copy(
-                src_ref=y.at[n, pl.ds(j * block, block)], dst_ref=y_in.at[n, j - 1],
-                send_sem=ya_s.at[n, j - 1], recv_sem=ya_r.at[n, j - 1],
-                device_id=expert_peer(ne - j), device_id_type=MESH))
-            sent[-1].start()
-        y_copies.append(sent)
+        if low == 2:
+            y_copies.append(pltpu.make_async_remote_copy(
+                src_ref=y.at[n, pl.ds(near, near)], dst_ref=y_in.at[n],
+                send_sem=ya_s.at[n], recv_sem=ya_r.at[n],
+                device_id=pair_peer(), device_id_type=MESH))
+            y_copies[-1].start()
         if n > 0:
-            forward(n - 1)
-    forward(down_n - 1)
+            far_step(n - 1)
+        if n > 1:
+            batch_step(n - 2)
+    far_step(down_n - 1)
+    for n in range(max(down_n - 2, 0), down_n):
+        batch_step(n)
     for n in range(down_n):
         finish(n)
 
@@ -254,6 +308,7 @@
     hid = w_gate.shape[2]
     own_rows = slots // ne
     block = nb * own_rows
+    high_n = ne // 2 if ne % 2 == 0 else ne
     wo_n = dim // chunk_of(dim, 1024)
     hid_n = hid // chunk_of(hid, 256)
     down_n = dim // chunk_of(dim, 1024)
@@ -284,24 +339,26 @@
             pltpu.VMEM((slots * heads, length), f32),
             pltpu.VMEM((slots * heads, width), f32),
             pltpu.VMEM((slots * heads, width), f32),
-            pltpu.VMEM((ne, own_rows, dim), bf),
+            pltpu.VMEM((wo_n, ne, own_rows, dim // wo_n), bf),
             pltpu.VMEM((ne, own_rows, dim), f32),
-            pltpu.VMEM((ne - 1, own_rows, dim), bf),
-            pltpu.VMEM((own_rows, ext), bf),
-            pltpu.VMEM((nb - 1, own_rows, ext), bf),
-            pltpu.VMEM((block, ext), f32),
+            pltpu.VMEM((wo_n, ne - 1, own_rows, dim // wo_n), bf),
+            pltpu.VMEM((ne, nb, own_rows, ext), bf),
+            pltpu.VMEM((ne * block, ext), f32),
             pltpu.VMEM((ne * block, ext), bf),
             pltpu.VMEM((ne * block, hid), bf),
             pltpu.VMEM((down_n, ne * block, down_c), bf),
-            pltpu.VMEM((down_n, ne - 1, block, down_c), bf),
+            pltpu.VMEM((down_n, high_n * block, down_c), bf),
+            pltpu.VMEM((down_n, block, down_c), f32),
+            pltpu.VMEM((down_n, high_n, block, down_c), bf),
+            pltpu.VMEM((down_n, high_n, block, down_c), bf),
             pltpu.VMEM((own_rows, dim), f32),
             pltpu.VMEM((down_n, nb - 1, own_rows, down_c), bf),
             pltpu.VMEM((down_n, nb - 1, own_rows, down_c), bf),
             pltpu.VMEM((own_rows, dim), f32),
             dma((8,)), dma((wo_n,)), dma((hid_n,)), dma((hid_n,)), dma((down_n,)),
-            dma((ne - 1,)), dma((ne - 1,)), dma((nb - 1,)), dma((nb - 1,)),
-            dma((ne - 1,)), dma((ne - 1,)),
-            dma((down_n, ne - 1)), dma((down_n, ne - 1)),
+            dma((wo_n, ne - 1)), dma((wo_n, ne - 1)), dma((nb - 1,)), dma((nb - 1,)),
+            dma((high_n, nb)), dma((high_n, nb)), dma((high_n, nb)), dma((high_n, nb)),
+            dma((down_n,)), dma((down_n,)), dma((down_n, high_n)), dma((down_n, high_n)),
             dma((down_n, nb - 1)), dma((down_n, nb - 1)),
         ],
         compiler_params=pltpu.CompilerParams(

time: 46.1 us -> 42.9 us (0.931)
  Pallas kernels: 44.5 us -> 41.3 us
    pallas_call x1, Pallas kernels: 44.5 us -> 41.3 us  [body(): pl.pallas_call(functools.partial(kernel, nb, ne), out_shape=jax.ShapeDtyp...]
where the time goes in v3:
time: 42.9 us; the launch traced here: 42.7 us
  Pallas kernels  41.3 us (96%)
  local copies, waits for them, and re-layouts  1.39 us (3%)
    pallas_call x1, Pallas kernels, body(): pl.pallas_call(functools.partial(kernel, nb, ne), out_shape=jax.ShapeDtyp...  41.3 us
    unnamed x1, local copies, waits for them, and re-layouts  1.39 us

profile of v3, /device:TPU:0, one launch (start us, length us, event | category | flops | bytes accessed | tf_op | source)
XLA Modules:
  0.0 42.7 jit_solution(6427510992616139978)
XLA Ops:
  0.0 41.3 %shard_map.145 = bf16[4,4096]{1,0:T(4,128)(2,1)} custom-call(s32[16]{0:T(128)} %lens.1, s32[16]{0:T(128)} %fresh.1, s32[2,16]{1,0:T(2,128)} %bitcast.9, bf16[16,4096]{1,0:T(8,128)(2,1)} %resid_h.1, bf16[16,4,128]{2,1,0:T(4,128)(2,1)} %q_h.1, bf16[1,16,128]{2,1,0:T(8,128)(2,1)} %bitcast.7, bf16[1,16,128]{2,1,0:T(8,128)(2,1)} %bitcast.8, ...), custom_call_target="tpu_custom_call" | custom-call | tf_op jit(solution)/shard_map/pallas_call | solution.py:321
  41.3 1.4 %copy.17 = bf16[4,4096]{1,0:T(4,128)(2,1)} copy(bf16[4,4096]{1,0:T(4,128)(2,1)} %shard_map.145) | data formatting | bytes 65536

commit v4 on v3

--- a/solution.py
+++ b/solution.py
@@ -309,9 +309,9 @@
     own_rows = slots // ne
     block = nb * own_rows
     high_n = ne // 2 if ne % 2 == 0 else ne
-    wo_n = dim // chunk_of(dim, 1024)
-    hid_n = hid // chunk_of(hid, 256)
-    down_n = dim // chunk_of(dim, 1024)
+    wo_n = dim // chunk_of(dim, 2048)
+    hid_n = hid // chunk_of(hid, 512)
+    down_n = dim // chunk_of(dim, 2048)
     down_c = dim // down_n
     bf, f32 = jnp.bfloat16, jnp.float32
     smem = pl.BlockSpec(memory_space=pltpu.SMEM)

time: 42.9 us -> 40.9 us (0.953)
  Pallas kernels: 41.3 us -> 39.3 us
    pallas_call x1, Pallas kernels: 41.3 us -> 39.3 us  [body(): pl.pallas_call(functools.partial(kernel, nb, ne), out_shape=jax.ShapeDtyp...]
where the time goes in v4:
time: 40.9 us; the launch traced here: 40.7 us
  Pallas kernels  39.3 us (96%)
  local copies, waits for them, and re-layouts  1.39 us (3%)
    pallas_call x1, Pallas kernels, body(): pl.pallas_call(functools.partial(kernel, nb, ne), out_shape=jax.ShapeDtyp...  39.3 us
    unnamed x1, local copies, waits for them, and re-layouts  1.39 us

profile of v4, /device:TPU:0, one launch (start us, length us, event | category | flops | bytes accessed | tf_op | source)
XLA Modules:
  0.0 40.7 jit_solution(4738883975599419306)
XLA Ops:
  0.0 39.3 %shard_map.145 = bf16[4,4096]{1,0:T(4,128)(2,1)} custom-call(s32[16]{0:T(128)} %lens.1, s32[16]{0:T(128)} %fresh.1, s32[2,16]{1,0:T(2,128)} %bitcast.9, bf16[16,4096]{1,0:T(8,128)(2,1)} %resid_h.1, bf16[16,4,128]{2,1,0:T(4,128)(2,1)} %q_h.1, bf16[1,16,128]{2,1,0:T(8,128)(2,1)} %bitcast.7, bf16[1,16,128]{2,1,0:T(8,128)(2,1)} %bitcast.8, ...), custom_call_target="tpu_custom_call" | custom-call | tf_op jit(solution)/shard_map/pallas_call | solution.py:321
  39.3 1.4 %copy.17 = bf16[4,4096]{1,0:T(4,128)(2,1)} copy(bf16[4,4096]{1,0:T(4,128)(2,1)} %shard_map.145) | data formatting | bytes 65536
